TPU v7x, 256 devices: a whole 4x4x8 slice. The times are simulated.
256 devices in a mesh: row: 16 (over z_hi, y, core), col: 16 (over z_lo, x).
Axes of the slice: x: 4, y: 4, z: 8 (z_hi: 2, z_lo: 4; z = z_hi * 4 + z_lo), core: 2. Of those that a mesh axis runs over, the one named last changes fastest.
Arguments:
- features: bfloat16 [65536, 128], P(('col', 'row')), may hold values from -6 to 6
- weight: bfloat16 [128, 128], replicated, may hold values from -0.5 to 0.5
- tiles: bfloat16 [16, 16, 352, 128, 128], P('row', 'col'), may hold values from -0.0546875 to 0.0546875
- tile_slots: int32 [16, 16, 352], P('row', 'col'), may hold values from 0 to 1023, as said below
- tile_counts: int32 [16, 16], P('row', 'col'), may hold values from 44 to 352, as said below
- cotangent: bfloat16 [65536, 128], P(('row', 'col')), may hold values from -6 to 6
Outputs:
- hidden: bfloat16 [65536, 128], P(('row', 'col'))
- feature_grad: bfloat16 [65536, 128], P(('col', 'row'))
- weight_grad: float32 [128, 128], replicated
Inputs may be any that keep to these rules, and one draw needn't show every extreme that they name: `tile_slots`: the slots of one block are distinct. `tile_counts`: some block has all 352 slots live.
All inputs are finite; a program needn't handle non-finite values.
Results may differ from a plain program's by a relative error of at most 0.006.
Values may be sent and summed in bfloat16 or wider, within the bound.
A program may use at most 128 MiB of HBM per device.

v0:
```python
import math
import jax
import jax.numpy as jnp
from jax import lax
from jax.sharding import PartitionSpec as P


def silu_grad(values):
    sig = jax.nn.sigmoid(values)
    return sig * (1.0 + values * (1.0 - sig))


def body(features, weight, tiles, tile_slots, tile_counts, cotangent):
    tile_vals = tiles[0, 0]
    slot_ids = tile_slots[0, 0]
    live_count = tile_counts[0, 0]
    tile_size = tile_vals.shape[-1]
    share_rows = features.shape[0]
    width = features.shape[1]
    slot_total = slot_ids.shape[0]
    row_count = lax.axis_size("row")
    col_count = lax.axis_size("col")
    tile_rows = share_rows * col_count // tile_size
    tile_cols = share_rows * row_count // tile_size
    col_index = lax.axis_index("col")
    projected = jnp.dot(features, weight, preferred_element_type=jnp.float32).astype(jnp.bfloat16)
    proj_block = lax.all_gather(projected, "row", axis=0, tiled=True)
    is_live = jnp.arange(slot_total, dtype=jnp.int32) < live_count
    gathered = proj_block.reshape(tile_cols, tile_size, width)[slot_ids % tile_cols]
    products = jnp.einsum("tij,tjf->tif", tile_vals, gathered, preferred_element_type=jnp.float32)
    fwd_targets = jnp.where(is_live, slot_ids // tile_cols, tile_rows)
    partial_value = jax.ops.segment_sum(products, fwd_targets, tile_rows + 1)[:tile_rows].reshape(
        tile_rows * tile_size, width
    )
    summed = lax.psum(partial_value, "col")
    own_rows = lax.dynamic_slice_in_dim(summed, col_index * share_rows, share_rows, 0)
    hidden = jax.nn.silu(own_rows).astype(jnp.bfloat16)
    cot_block = lax.all_gather(cotangent, "col", axis=0, tiled=True)
    grad_block = (cot_block.astype(jnp.float32) * silu_grad(summed)).astype(jnp.bfloat16)
    grad_tiles = grad_block.reshape(tile_rows, tile_size, width)[slot_ids // tile_cols]
    back_products = jnp.einsum(
        "tji,tjf->tif", tile_vals, grad_tiles, preferred_element_type=jnp.float32
    )
    back_targets = jnp.where(is_live, slot_ids % tile_cols, tile_cols)
    back_partial = jax.ops.segment_sum(back_products, back_targets, tile_cols + 1)[
        :tile_cols
    ].reshape(tile_cols * tile_size, width)
    grad_proj = lax.psum_scatter(back_partial, "row", scatter_dimension=0, tiled=True).astype(
        jnp.bfloat16
    )
    feature_grad = jnp.dot(grad_proj, weight.T, preferred_element_type=jnp.float32).astype(
        jnp.bfloat16
    )
    weight_term = jnp.dot(features.T, grad_proj, preferred_element_type=jnp.float32)
    node_total = share_rows * row_count * col_count
    weight_grad = lax.psum(weight_term, ("row", "col")) / math.sqrt(node_total)
    return (hidden, feature_grad, weight_grad)


def solution(mesh):
    placed = (
        P(("col", "row"), None),
        P(),
        P("row", "col", None, None, None),
        P("row", "col", None),
        P("row", "col"),
        P(("row", "col"), None),
    )
    return jax.shard_map(
        body,
        mesh=mesh,
        in_specs=placed,
        out_specs=(P(("row", "col"), None), P(("col", "row"), None), P()),
        check_vma=False,
    )
```

profile of v0, /device:TPU:1, one launch (start us, length us, event | category | flops | bytes accessed | tf_op | source)
XLA Modules:
  0.0 771.6 jit_solution(9133756063964806921)
XLA Ops:
  7.2 0.0 all-gather.3.cloned.1.call-start
  7.2 0.8 copy-done
  8.0 1.5 convolution_convert_fusion.1
  9.6 0.0 all-gather.5.cloned.1.call-start
  9.6 0.7 all-gather.5.cloned.1.call-update
  10.3 0.0 all-reduce.3.cloned.1.call-start
  11.0 0.7 fusion.15
  11.7 0.7 fusion.13
  12.4 58.8 %all-gather.3.cloned.1.call-done = bf16[4096,128]{1,0:T(8,128)(2,1)} async-done(((bf16[256,128]{1,0:T(8,128)(2,1)}), bf16[4096,128]{1,0:T(8,128)(2,1)}) %all-gather.3.cloned.1.call-update) | async-done | bytes 1048592 | tf_op jit(solution)/shard_map/all_gather | solution.py:27
  71.3 12.2 %gather_fusion = bf16[352,128,128]{2,1,0:T(8,128)(2,1)} fusion(bf16[32,128,128]{2,1,0:T(8,128)(2,1)} %bitcast.41, s32[1024]{0:T(1024)S(1)} %pad_clamp_fusion.1), kind=kCustom, calls=%fused_computation | custom fusion | bytes 23070080 | tf_op jit(solution)/shard_map/gather | solution.py:29
  83.5 20.6 %fusion.4 = f32[352,128,128]{1,2,0:T(8,128)} fusion(bf16[352,128,128]{2,1,0:T(8,128)(2,1)} %gather_fusion, bf16[1,1,352,128,128]{4,3,2,1,0:T(8,128)(2,1)} %param.8), kind=kOutput, calls=%fused_computation.8 | convolution fusion | flops 1476395008 | bytes 46137344 | tf_op jit(solution)/shard_map/tij,tjf->tif/dot_general | solution.py:30
  104.1 23.5 %copy.13 = f32[352,128,128]{2,1,0:T(8,128)} copy(f32[352,128,128]{1,2,0:T(8,128)} %fusion.4) | data formatting | bytes 46137344 | tf_op jit(solution)/shard_map/tij,tjf->tif/dot_general | solution.py:30
  127.6 0.2 broadcast.191.clone
  127.8 46.0 %scatter_fusion = f32[33,128,128]{2,1,0:T(8,128)S(1)} fusion(f32[33,128,128]{2,1,0:T(8,128)S(1)} %broadcast.191.clone, s32[352]{0:T(512)S(1)} %get-tuple-element.10, f32[352,128,128]{2,1,0:T(8,128)} %copy.13), kind=kCustom, calls=%fused_computation.2 | custom fusion | flops 5767168 | bytes 69207424 | tf_op jit(solution)/shard_map/scatter-add | solution.py:32
  173.9 1.5 slice.12
  175.4 0.2 reduce-scatter.2.cloned.1.call-start
  175.7 153.0 %all-reduce.3.cloned.1.call-done = f32[4096,128]{1,0:T(8,128)} async-done(((f32[4096,128]{1,0:T(8,128)}), f32[4096,128]{1,0:T(8,128)}) %all-reduce.3.cloned.1.call-update) | async-done | bytes 2097168 | tf_op jit(solution)/shard_map/psum | solution.py:35
  328.6 2.6 multiply_convert_fusion
  331.3 11.0 %gather_fusion.1 = bf16[352,128,128]{2,1,0:T(8,128)(2,1)} fusion(bf16[32,128,128]{2,1,0:T(8,128)(2,1)S(1)} %bitcast.40, s32[1024]{0:T(1024)S(1)} %pad_clamp_fusion), kind=kCustom, calls=%fused_computation.1 | custom fusion | bytes 23070080 | tf_op jit(solution)/shard_map/gather | solution.py:40
  342.3 14.4 %fusion.7 = f32[352,128,128]{1,2,0:T(8,128)} fusion(bf16[352,128,128]{2,1,0:T(8,128)(2,1)} %gather_fusion.1, bf16[1,1,352,128,128]{4,3,2,1,0:T(8,128)(2,1)} %param.8), kind=kOutput, calls=%fused_computation.9 | convolution fusion | flops 1476395008 | bytes 46137344 | tf_op jit(solution)/shard_map/tji,tjf->tif/dot_general | solution.py:41
  356.7 23.5 %copy.15 = f32[352,128,128]{2,1,0:T(8,128)} copy(f32[352,128,128]{1,2,0:T(8,128)} %fusion.7) | data formatting | bytes 46137344 | tf_op jit(solution)/shard_map/tji,tjf->tif/dot_general | solution.py:41
  380.2 0.2 broadcast.191
  380.4 46.0 %scatter_fusion.1 = f32[33,128,128]{2,1,0:T(8,128)S(1)} fusion(f32[33,128,128]{2,1,0:T(8,128)S(1)} %broadcast.191, s32[352]{0:T(512)S(1)} %get-tuple-element.11, f32[352,128,128]{2,1,0:T(8,128)} %copy.15), kind=kCustom, calls=%fused_computation.3 | custom fusion | flops 5767168 | bytes 69207424 | tf_op jit(solution)/shard_map/scatter-add | solution.py:45
  426.4 1.5 slice.13
  428.0 0.0 all-reduce.5.cloned.1.call-start
  428.0 1.6 multiply_convert_fusion.1
  429.6 92.6 %reduce-scatter.2.cloned.1.call-done = f32[256,128]{1,0:T(8,128)} async-done(((f32[4096,128]{1,0:T(8,128)}), f32[256,128]{1,0:T(8,128)}) %reduce-scatter.2.cloned.1.call-update) | async-done | bytes 131088 | tf_op jit(solution)/shard_map/reduce_scatter | solution.py:48
  522.2 1.7 convolution_bitcast_fusion
  524.0 1.7 convolution_convert_fusion
  525.7 237.9 %all-reduce.5.cloned.1.call-done = f32[128,128]{0,1:T(8,128)} async-done(((f32[128,128]{0,1:T(8,128)}), f32[128,128]{0,1:T(8,128)}) %all-reduce.5.cloned.1.call-update) | async-done | bytes 65552 | tf_op jit(solution)/shard_map/psum | solution.py:56
  763.5 0.8 broadcast_multiply_fusion
  764.4 0.7 copy.16
  (10 shorter events, 0.1 us)
Async XLA Ops:
  7.2 0.8 copy-start
  7.2 64.1 %all-gather.3.cloned.1.call-start = ((), (), s32[]{:S(2)}) async-start(), calls=%async_computation.1 | async-start | bytes 1114112 | tf_op jit(solution)/shard_map/all_gather | solution.py:27
  9.6 166.1 %all-gather.5.cloned.1.call-start = ((), (), s32[]{:S(2)}) async-start(), calls=%async_computation.3 | async-start | bytes 1114112 | tf_op jit(solution)/shard_map/all_gather | solution.py:38
  10.3 318.3 %all-reduce.3.cloned.1.call-start = ((), (), s32[]{:S(2)}) async-start(), calls=%async_computation.2 | async-start | bytes 4194304 | tf_op jit(solution)/shard_map/psum | solution.py:35
  175.4 346.8 %reduce-scatter.2.cloned.1.call-start = ((), (), s32[]{:S(2)}) async-start(), calls=%async_computation.4 | async-start | bytes 2228224 | tf_op jit(solution)/shard_map/reduce_scatter | solution.py:48
  380.4 143.5 %copy-start.1 = (bf16[128,128]{1,0:T(8,128)(2,1)S(1)}, bf16[128,128]{1,0:T(8,128)(2,1)}, u32[]{:S(2)}) copy-start(bf16[128,128]{1,0:T(8,128)(2,1)} %param.7) | copy-start | bytes 98308
  428.0 335.5 %all-reduce.5.cloned.1.call-start = ((), (), s32[]{:S(2)}) async-start(), calls=%async_computation.5 | async-start | bytes 131072 | tf_op jit(solution)/shard_map/psum | solution.py:56
Sparse Core Ops, SparseCore 0:
  11.3 59.9 all-gather.2
  73.1 65.9 all-gather.4
  175.5 153.0 all-reduce.2
  428.1 94.0 reduce-scatter.1
  528.1 235.3 all-reduce.4
where the time goes:
time: 774 us; the launch traced here: 772 us
  waiting for transfers between devices  543 us (70%)
  other arithmetic  98.5 us (13%)
  local copies, waits for them, and re-layouts  75.1 us (10%)
  matrix products  40 us (5%)
  between operations  14.5 us (2%)
    psum x1, waiting for transfers between devices, body(): weight_grad = lax.psum(weight_term, ('row', 'col')) / math.sqrt(node_total)  238 us
    psum x1, waiting for transfers between devices, body(): summed = lax.psum(partial_value, 'col')  153 us
    reduce_scatter x1, waiting for transfers between devices, body(): lax.psum_scatter(back_partial, 'row', scatter_dimension=0, tiled=True)  92.6 us
    all_gather x1, waiting for transfers between devices, body(): proj_block = lax.all_gather(projected, 'row', axis=0, tiled=True)  58.8 us
    scatter-add x1, other arithmetic, body(): jax.ops.segment_sum(products, fwd_targets, tile_rows + 1)[:tile_rows]  46 us
    scatter-add x1, other arithmetic, body(): jax.ops.segment_sum(back_products, back_targets, tile_cols + 1)[:tile_cols]  46 us
    dot_general x1, local copies, waits for them, and re-layouts, body(): jnp.einsum('tij,tjf->tif', tile_vals, gathered, preferred_element_type=jn...  23.5 us
    dot_general x1, local copies, waits for them, and re-layouts, body(): jnp.einsum('tji,tjf->tif', tile_vals, grad_tiles, preferred_element_type=...  23.5 us
  transfers between devices with their start and end apart: 5, of which 4 were waited for; matrix products, arithmetic and copies ran while one was open for 14% of the time, Pallas kernels for 0%

commit v1 on v0

--- a/solution.py
+++ b/solution.py
@@ -53,7 +53,7 @@
     )
     weight_term = jnp.dot(features.T, grad_proj, preferred_element_type=jnp.float32)
     node_total = share_rows * row_count * col_count
-    weight_grad = lax.psum(weight_term, ("row", "col")) / math.sqrt(node_total)
+    weight_grad = lax.psum(lax.psum(weight_term, "row"), "col") / math.sqrt(node_total)
     return (hidden, feature_grad, weight_grad)
 
 

time: 774 us -> 847 us (1.094)
  waiting for transfers between devices: 543 us -> 609 us
    psum x1 -> x2, waiting for transfers between devices: 238 us -> 302 us  [the longest x1 161 us: body(): lax.psum(weight_term, 'row')]
  transfers between devices with their start and end apart: 5 -> 6, of which waited for: 4 -> 5; matrix products, arithmetic and copies ran while one was open for 14% -> 13% of each run, Pallas kernels for 0% -> 0%
where the time goes in v1:
time: 847 us; the launch traced here: 838 us
  waiting for transfers between devices  609 us (72%)
  other arithmetic  98.5 us (12%)
  local copies, waits for them, and re-layouts  75.1 us (9%)
  matrix products  40 us (5%)
  between operations  14.8 us (2%)
    psum x1, waiting for transfers between devices, body(): lax.psum(weight_term, 'row')  161 us
    psum x1, waiting for transfers between devices, body(): summed = lax.psum(partial_value, 'col')  153 us
    psum x1, waiting for transfers between devices, body(): lax.psum(lax.psum(weight_term, 'row'), 'col') / math.sqrt(node_total)  141 us
    reduce_scatter x1, waiting for transfers between devices, body(): lax.psum_scatter(back_partial, 'row', scatter_dimension=0, tiled=True)  94.2 us
    all_gather x1, waiting for transfers between devices, body(): proj_block = lax.all_gather(projected, 'row', axis=0, tiled=True)  58.8 us
    scatter-add x1, other arithmetic, body(): jax.ops.segment_sum(products, fwd_targets, tile_rows + 1)[:tile_rows]  46 us
    scatter-add x1, other arithmetic, body(): jax.ops.segment_sum(back_products, back_targets, tile_cols + 1)[:tile_cols]  46 us
    dot_general x1, local copies, waits for them, and re-layouts, body(): jnp.einsum('tij,tjf->tif', tile_vals, gathered, preferred_element_type=jn...  23.5 us
  transfers between devices with their start and end apart: 6, of which 5 were waited for; matrix products, arithmetic and copies ran while one was open for 13% of the time, Pallas kernels for 0%

profile of v1, /device:TPU:1, one launch (start us, length us, event | category | flops | bytes accessed | tf_op | source)
XLA Modules:
  0.0 837.8 jit_solution(10920760001872046439)
XLA Ops:
  7.2 0.8 copy-done
  8.0 1.5 convolution_convert_fusion.1
  9.6 0.0 all-gather.5.cloned.1.call-start
  9.6 0.7 all-gather.5.cloned.1.call-update
  11.0 0.7 fusion.15
  11.7 0.7 fusion.13
  12.4 58.8 %all-gather.3.cloned.1.call-done = bf16[4096,128]{1,0:T(8,128)(2,1)} async-done(((bf16[256,128]{1,0:T(8,128)(2,1)}), bf16[4096,128]{1,0:T(8,128)(2,1)}) %all-gather.3.cloned.1.call-update) | async-done | bytes 1048592 | tf_op jit(solution)/shard_map/all_gather | solution.py:27
  71.3 12.2 %gather_fusion = bf16[352,128,128]{2,1,0:T(8,128)(2,1)} fusion(bf16[32,128,128]{2,1,0:T(8,128)(2,1)} %bitcast.41, s32[1024]{0:T(1024)S(1)} %pad_clamp_fusion.1), kind=kCustom, calls=%fused_computation | custom fusion | bytes 23070080 | tf_op jit(solution)/shard_map/gather | solution.py:29
  83.5 20.6 %fusion.4 = f32[352,128,128]{1,2,0:T(8,128)} fusion(bf16[352,128,128]{2,1,0:T(8,128)(2,1)} %gather_fusion, bf16[1,1,352,128,128]{4,3,2,1,0:T(8,128)(2,1)} %param.8), kind=kOutput, calls=%fused_computation.8 | convolution fusion | flops 1476395008 | bytes 46137344 | tf_op jit(solution)/shard_map/tij,tjf->tif/dot_general | solution.py:30
  104.1 23.5 %copy.13 = f32[352,128,128]{2,1,0:T(8,128)} copy(f32[352,128,128]{1,2,0:T(8,128)} %fusion.4) | data formatting | bytes 46137344 | tf_op jit(solution)/shard_map/tij,tjf->tif/dot_general | solution.py:30
  127.6 0.2 broadcast.191.clone
  127.8 46.0 %scatter_fusion = f32[33,128,128]{2,1,0:T(8,128)S(1)} fusion(f32[33,128,128]{2,1,0:T(8,128)S(1)} %broadcast.191.clone, s32[352]{0:T(512)S(1)} %get-tuple-element.10, f32[352,128,128]{2,1,0:T(8,128)} %copy.13), kind=kCustom, calls=%fused_computation.2 | custom fusion | flops 5767168 | bytes 69207424 | tf_op jit(solution)/shard_map/scatter-add | solution.py:32
  173.9 1.5 slice.12
  175.4 0.2 reduce-scatter.2.cloned.1.call-start
  175.7 153.0 %all-reduce.4.cloned.1.call-done = f32[4096,128]{1,0:T(8,128)} async-done(((f32[4096,128]{1,0:T(8,128)}), f32[4096,128]{1,0:T(8,128)}) %all-reduce.4.cloned.1.call-update) | async-done | bytes 2097168 | tf_op jit(solution)/shard_map/psum | solution.py:35
  328.6 2.6 multiply_convert_fusion
  331.3 11.0 %gather_fusion.1 = bf16[352,128,128]{2,1,0:T(8,128)(2,1)} fusion(bf16[32,128,128]{2,1,0:T(8,128)(2,1)S(1)} %bitcast.40, s32[1024]{0:T(1024)S(1)} %pad_clamp_fusion), kind=kCustom, calls=%fused_computation.1 | custom fusion | bytes 23070080 | tf_op jit(solution)/shard_map/gather | solution.py:40
  342.3 14.4 %fusion.7 = f32[352,128,128]{1,2,0:T(8,128)} fusion(bf16[352,128,128]{2,1,0:T(8,128)(2,1)} %gather_fusion.1, bf16[1,1,352,128,128]{4,3,2,1,0:T(8,128)(2,1)} %param.8), kind=kOutput, calls=%fused_computation.9 | convolution fusion | flops 1476395008 | bytes 46137344 | tf_op jit(solution)/shard_map/tji,tjf->tif/dot_general | solution.py:41
  356.7 23.5 %copy.15 = f32[352,128,128]{2,1,0:T(8,128)} copy(f32[352,128,128]{1,2,0:T(8,128)} %fusion.7) | data formatting | bytes 46137344 | tf_op jit(solution)/shard_map/tji,tjf->tif/dot_general | solution.py:41
  380.2 0.2 broadcast.191
  380.4 46.0 %scatter_fusion.1 = f32[33,128,128]{2,1,0:T(8,128)S(1)} fusion(f32[33,128,128]{2,1,0:T(8,128)S(1)} %broadcast.191, s32[352]{0:T(512)S(1)} %get-tuple-element.11, f32[352,128,128]{2,1,0:T(8,128)} %copy.15), kind=kCustom, calls=%fused_computation.3 | custom fusion | flops 5767168 | bytes 69207424 | tf_op jit(solution)/shard_map/scatter-add | solution.py:45
  426.4 1.5 slice.13
  428.0 0.0 all-reduce.6.cloned.1.call-start
  428.0 94.2 %reduce-scatter.2.cloned.1.call-done = f32[256,128]{1,0:T(8,128)} async-done(((f32[4096,128]{1,0:T(8,128)}), f32[256,128]{1,0:T(8,128)}) %reduce-scatter.2.cloned.1.call-update) | async-done | bytes 131088 | tf_op jit(solution)/shard_map/reduce_scatter | solution.py:48
  522.2 1.7 convolution_bitcast_fusion
  523.9 0.0 all-reduce.8.cloned.1.call-start
  524.0 1.6 multiply_convert_fusion.1
  525.6 161.4 %all-reduce.6.cloned.1.call-done = f32[128,128]{0,1:T(8,128)} async-done(((f32[128,128]{0,1:T(8,128)}), f32[128,128]{0,1:T(8,128)}) %all-reduce.6.cloned.1.call-update) | async-done | bytes 65552 | tf_op jit(solution)/shard_map/psum | solution.py:56
  687.1 1.7 convolution_convert_fusion
  688.8 140.6 %all-reduce.8.cloned.1.call-done = f32[128,128]{0,1:T(8,128)} async-done(((f32[128,128]{0,1:T(8,128)}), f32[128,128]{0,1:T(8,128)}) %all-reduce.8.cloned.1.call-update) | async-done | bytes 65552 | tf_op jit(solution)/shard_map/psum | solution.py:56
  829.4 0.8 broadcast_multiply_fusion
  830.2 0.7 copy.16
  (13 shorter events, 0.2 us)
Async XLA Ops:
  7.2 0.8 copy-start
  7.2 64.1 %all-gather.3.cloned.1.call-start = ((), (), s32[]{:S(2)}) async-start(), calls=%async_computation.1 | async-start | bytes 1114112 | tf_op jit(solution)/shard_map/all_gather | solution.py:27
  9.6 166.1 %all-gather.5.cloned.1.call-start = ((), (), s32[]{:S(2)}) async-start(), calls=%async_computation.3 | async-start | bytes 1114112 | tf_op jit(solution)/shard_map/all_gather | solution.py:38
  10.3 318.3 %all-reduce.4.cloned.1.call-start = ((), (), s32[]{:S(2)}) async-start(), calls=%async_computation.2 | async-start | bytes 4194304 | tf_op jit(solution)/shard_map/psum | solution.py:35
  175.4 346.8 %reduce-scatter.2.cloned.1.call-start = ((), (), s32[]{:S(2)}) async-start(), calls=%async_computation.4 | async-start | bytes 2228224 | tf_op jit(solution)/shard_map/reduce_scatter | solution.py:48
  380.4 306.6 %copy-start.1 = (bf16[128,128]{1,0:T(8,128)(2,1)S(1)}, bf16[128,128]{1,0:T(8,128)(2,1)}, u32[]{:S(2)}) copy-start(bf16[128,128]{1,0:T(8,128)(2,1)} %param.7) | copy-start | bytes 98308
  428.0 259.1 %all-reduce.6.cloned.1.call-start = ((), (), s32[]{:S(2)}) async-start(), calls=%async_computation.5 | async-start | bytes 131072 | tf_op jit(solution)/shard_map/psum | solution.py:56
  523.9 305.4 %all-reduce.8.cloned.1.call-start = ((), (), s32[]{:S(2)}) async-start(), calls=%async_computation.6 | async-start | bytes 131072 | tf_op jit(solution)/shard_map/psum | solution.py:56
Sparse Core Ops, SparseCore 0:
  11.3 59.9 all-gather.2
  73.1 65.9 all-gather.4
  175.5 153.0 all-reduce.3
  428.1 94.0 reduce-scatter.1
  525.2 161.7 all-reduce.5
  689.7 139.6 all-reduce.7
